TPU v7x, 32 devices: a whole 2x2x4 slice. The times are simulated.
32 devices in a mesh: seq: 8 (over z, y), span: 4 (over x, core).
Axes of the slice: x: 2, y: 2, z: 4, core: 2. Of those that a mesh axis runs over, the one named last changes fastest.
Arguments:
- inputs: bfloat16 [8, 512, 768], P('seq', 'span'), may hold values from -6 to 6
- norm_gain: float32 [768], replicated, may hold values from 0.1 to 1.9
- z_weight: bfloat16 [768, 1536], P(('seq', 'span')), may hold values from -0.21875 to 0.21875
- xbc_weight: bfloat16 [768, 1792], P(('seq', 'span')), may hold values from -0.21875 to 0.21875
- dt_weight: bfloat16 [768, 24], P(('seq', 'span')), may hold values from -0.21875 to 0.21875
- conv_weight: float32 [4, 1792], replicated, may hold values from -3 to 3
- conv_bias: float32 [1792], replicated, may hold values from -3 to 3
- dt_bias: float32 [24], replicated, may hold values from -6 to -1
- a_log: float32 [24], replicated, may hold values from -1 to 1.5
- skip_gain: float32 [24], replicated, may hold values from 0.5 to 1.5
- gate_gain: float32 [1536], replicated, may hold values from 0.1 to 1.9
- out_weight: bfloat16 [1536, 768], P(('seq', 'span')), may hold values from -0.15625 to 0.15625
- segments: int32 [8, 512], P('seq', 'span'), may hold values from 0 to 3, never falling along the last dimension, each value on 1 to 256 neighbouring positions
- cotangent: bfloat16 [8, 512, 768], P('seq', 'span'), may hold values from -6 to 6
Outputs:
- output: bfloat16 [8, 512, 768], P('seq', 'span')
- input_grad: float32 [8, 512, 768], P('seq', 'span')
- norm_gain_grad: float32 [768], replicated
- z_weight_grad: float32 [768, 1536], P(('seq', 'span'))
- xbc_weight_grad: float32 [768, 1792], P(('seq', 'span'))
- dt_weight_grad: float32 [768, 24], P(('seq', 'span'))
- conv_weight_grad: float32 [4, 1792], replicated
- conv_bias_grad: float32 [1792], replicated
- dt_bias_grad: float32 [24], replicated
- a_log_grad: float32 [24], replicated
- skip_gain_grad: float32 [24], replicated
- gate_gain_grad: float32 [1536], replicated
- out_weight_grad: float32 [1536, 768], P(('seq', 'span'))
Inputs may be any that keep to these rules, and one draw needn't show every extreme that they name: `segments`: within a sequence the numbers never fall; a document is one run of equal numbers, of 1 to 256 tokens.
All inputs are finite; a program needn't handle non-finite values.
Results may differ from a plain program's by a relative error of at most 0.0094.
Values may be sent and summed in bfloat16 or wider, within the bound.
A program may use at most 128 MiB of HBM per device.

v0:
```python
import jax
import jax.numpy as jnp
from jax import lax
from jax.sharding import PartitionSpec as P

DI = 1536
H = 24
P_SIZE = 64
N = 128
KW = 4
CH = 1792
EPSILON = 1e-05
HIGHEST = lax.Precision.HIGHEST
CONTRACT_LAST = (((1,), (1,)), ((), ()))
CONTRACT_FIRST = (((0,), (0,)), ((), ()))


def shifted(x, axis, by):
    devices = lax.axis_size(axis)
    pairs = [(i, i + by) for i in range(devices) if 0 <= i + by < devices]
    return lax.ppermute(x, axis, pairs)


def carried_in(part, axis, combine, identity, reverse):
    count = lax.axis_size(axis)
    place = lax.axis_index(axis)
    ahead = count - 1 - place if reverse else place
    gathered = jax.tree.map(lambda a: lax.all_gather(a, axis), part)
    state = jax.tree.map(lambda a, e: jnp.zeros_like(a) + jnp.asarray(e, a.dtype), part, identity)

    def one(turn, state):
        source = count - 1 - turn if reverse else turn
        return combine(
            state, jax.tree.map(lambda a: lax.dynamic_index_in_dim(a, source, 0, False), gathered)
        )

    return lax.fori_loop(0, ahead, one, state)


def input_norm(values, gain):
    scale = lax.rsqrt(jnp.mean(values * values, axis=-1, keepdims=True) + EPSILON)
    return values * scale * gain


def gated_norm(mixed, gate, gain):
    gated = mixed * jax.nn.silu(gate)
    scale = lax.rsqrt(jnp.mean(gated * gated, axis=-1, keepdims=True) + EPSILON)
    return gated * scale * gain


def conv_and_step(conv_in, edge, seg_now, seg_edge, conv_weight, conv_bias, dt_raw, dt_bias, a_log):
    taps = conv_weight.shape[0]
    length = conv_in.shape[0]
    padded = jnp.concatenate([edge, conv_in], axis=0)
    seg_all = jnp.concatenate([seg_edge, seg_now], axis=0)
    total = jnp.zeros_like(conv_in) + conv_bias
    for offset in range(taps):
        same = (seg_all[offset : offset + length] == seg_now).astype(jnp.float32)
        total = total + conv_weight[offset] * padded[offset : offset + length] * same[:, None]
    activated = jax.nn.silu(total)
    step_size = jax.nn.softplus(dt_raw + dt_bias)
    log_decay = -jnp.exp(a_log) * step_size
    return (activated, step_size, log_decay)


def scan_local(activated, step_size, log_decay, seg_now, seg_before, skip_gain):
    length = activated.shape[0]
    inner = activated[:, :DI].reshape(length, H, P_SIZE)
    in_state = activated[:, DI : DI + N]
    out_state = activated[:, DI + N :]
    cumul = jnp.cumsum(log_decay, axis=0)
    cum_heads = cumul.T
    later = lax.broadcasted_iota(jnp.int32, (length, length), 0)
    earlier = lax.broadcasted_iota(jnp.int32, (length, length), 1)
    allowed = (later >= earlier) & (seg_now[:, None] == seg_now[None, :])
    mask_three = allowed[None, :, :]
    spread = cum_heads[:, :, None] - cum_heads[:, None, :]
    decay = jnp.where(mask_three, jnp.exp(jnp.where(mask_three, spread, 0.0)), 0.0)
    intersection = jnp.dot(
        out_state, in_state.T, precision=HIGHEST, preferred_element_type=jnp.float32
    )
    mixing = intersection[None, :, :] * decay * step_size.T[:, None, :]
    result = jnp.einsum("hts,shp->thp", mixing, inner, precision=HIGHEST)
    result = result + skip_gain[None, :, None] * inner
    carried = jnp.exp(cumul) * (seg_now == seg_before).astype(jnp.float32)[:, None]
    tail = (
        jnp.exp(cumul[-1][None, :] - cumul)
        * (seg_now == seg_now[-1]).astype(jnp.float32)[:, None]
        * step_size
    )
    local_end = jnp.einsum("sh,shp,sn->hpn", tail, inner, in_state, precision=HIGHEST)
    return (result, local_end, carried)


def add_carry(result, carried, out_state, state_in):
    return result + carried[:, :, None] * jnp.einsum(
        "tn,hpn->thp", out_state, state_in, precision=HIGHEST
    )


def span_full(
    conv_in,
    edge,
    dt_raw,
    conv_weight,
    conv_bias,
    dt_bias,
    a_log,
    skip_gain,
    state_in,
    seg_now,
    seg_edge,
):
    activated, step_size, log_decay = conv_and_step(
        conv_in, edge, seg_now, seg_edge, conv_weight, conv_bias, dt_raw, dt_bias, a_log
    )
    result, local_end, carried = scan_local(
        activated, step_size, log_decay, seg_now, seg_edge[-1], skip_gain
    )
    mixed = add_carry(result, carried, activated[:, DI + N :], state_in)
    state_end = carried[-1][:, None, None] * state_in + local_end
    return (mixed.reshape(mixed.shape[0], DI), state_end)


def chain_states(earlier, later):
    return (earlier[0] * later[0], later[0][:, :, None, None] * earlier[1] + later[1])


def body(
    inputs,
    norm_gain,
    z_weight,
    xbc_weight,
    dt_weight,
    conv_weight,
    conv_bias,
    dt_bias,
    a_log,
    skip_gain,
    gate_gain,
    out_weight,
    segments,
    cotangent,
):
    seqs_here, span_len, width = inputs.shape
    rows = seqs_here * span_len
    flat = inputs.astype(jnp.float32).reshape(rows, width)
    normed = input_norm(flat, norm_gain).astype(jnp.bfloat16)
    pieces = (
        lax.all_gather(z_weight, ("seq", "span"), axis=0, tiled=True),
        lax.all_gather(xbc_weight, ("seq", "span"), axis=0, tiled=True),
        lax.all_gather(dt_weight, ("seq", "span"), axis=0, tiled=True),
    )
    columns = normed
    gate, conv_wide, dt_raw = tuple(
        (jnp.dot(columns, piece, preferred_element_type=jnp.float32) for piece in pieces)
    )
    conv_in = conv_wide.astype(jnp.bfloat16).reshape(seqs_here, span_len, CH)
    seg_wire = (segments[:, span_len - KW + 1 :] + 1).astype(jnp.bfloat16)
    edge, seg_edge = shifted((conv_in[:, span_len - KW + 1 :], seg_wire), "span", 1)
    conv_float = conv_in.astype(jnp.float32)
    edge_float = edge.astype(jnp.float32)
    seg_edge_float = seg_edge.astype(jnp.float32)
    seg_now = (segments + 1).astype(jnp.float32)
    dt_spans = dt_raw.reshape(seqs_here, span_len, H)
    prepare = jax.vmap(conv_and_step, in_axes=(0, 0, 0, 0, None, None, 0, None, None))
    activated, step_size, log_decay = prepare(
        conv_float,
        edge_float,
        seg_now,
        seg_edge_float,
        conv_weight,
        conv_bias,
        dt_spans,
        dt_bias,
        a_log,
    )
    local_scan = jax.vmap(scan_local, in_axes=(0, 0, 0, 0, 0, None))
    result, local_end, carried = local_scan(
        activated, step_size, log_decay, seg_now, seg_edge_float[:, -1], skip_gain
    )
    decay_total = carried[:, -1]
    identity = (jnp.ones_like(decay_total), jnp.zeros_like(local_end))
    state_in = carried_in((decay_total, local_end), "span", chain_states, identity, False)[1]
    out_state = activated[:, :, DI + N :]
    mixed = jax.vmap(add_carry)(result, carried, out_state, state_in).reshape(rows, DI)
    mix_bf = gated_norm(mixed, gate, gate_gain).astype(jnp.bfloat16)
    columns = mix_bf
    projected = jnp.dot(
        columns,
        lax.all_gather(out_weight, ("seq", "span"), axis=0, tiled=True),
        preferred_element_type=jnp.float32,
    )
    output = (flat + projected).astype(jnp.bfloat16).reshape(inputs.shape)
    grad_out = cotangent.reshape(rows, width)
    grad_mix = lax.dot_general(
        grad_out,
        lax.all_gather(out_weight, ("seq", "span"), axis=0, tiled=True),
        CONTRACT_LAST,
        preferred_element_type=jnp.float32,
    )
    unused_norm, gate_pull = jax.vjp(gated_norm, mixed, gate, gate_gain)
    grad_mixed, grad_gate, gate_gain_grad = gate_pull(grad_mix)
    grad_heads = grad_mixed.reshape(seqs_here, span_len, H, P_SIZE)
    summary = jnp.einsum("sth,sthp,stn->shpn", carried, grad_heads, out_state, precision=HIGHEST)
    state_grad = carried_in((decay_total, summary), "span", chain_states, identity, True)[1]

    def local_span(conv_a, edge_a, dt_a, weight_a, bias_a, dtb_a, alog_a, skip_a, state_a):
        batched = jax.vmap(span_full, in_axes=(0, 0, 0, None, None, None, None, None, 0, 0, 0))
        return batched(
            conv_a,
            edge_a,
            dt_a,
            weight_a,
            bias_a,
            dtb_a,
            alog_a,
            skip_a,
            state_a,
            seg_now,
            seg_edge_float,
        )

    unused_span, span_pull = jax.vjp(
        local_span,
        conv_float,
        edge_float,
        dt_spans,
        conv_weight,
        conv_bias,
        dt_bias,
        a_log,
        skip_gain,
        state_in,
    )
    grads = span_pull((grad_mixed.reshape(seqs_here, span_len, DI), state_grad))
    edge_back = shifted(grads[1], "span", -1)
    conv_grad = grads[0].at[:, span_len - KW + 1 :].add(edge_back)
    gate_bf = grad_gate.astype(jnp.bfloat16)
    conv_bf = conv_grad.reshape(rows, CH).astype(jnp.bfloat16)
    dt_bf = grads[2].reshape(rows, H).astype(jnp.bfloat16)
    grad_joined = jnp.concatenate([gate_bf, conv_bf, dt_bf], axis=1)
    out_full = lax.dot_general(mix_bf, grad_out, CONTRACT_FIRST, preferred_element_type=jnp.float32)
    in_full = lax.dot_general(
        normed, grad_joined, CONTRACT_FIRST, preferred_element_type=jnp.float32
    )
    out_weight_grad, in_owned = (
        lax.psum_scatter(out_full, ("seq", "span"), scatter_dimension=0, tiled=True),
        lax.psum_scatter(in_full, ("seq", "span"), scatter_dimension=0, tiled=True),
    )
    z_weight_grad = in_owned[:, :DI]
    xbc_weight_grad = in_owned[:, DI : DI + CH]
    dt_weight_grad = in_owned[:, DI + CH :]
    pieces = lax.all_gather((z_weight, xbc_weight, dt_weight), ("seq", "span"), axis=0, tiled=True)
    partial_sum = lax.dot_general(
        gate_bf, pieces[0], CONTRACT_LAST, preferred_element_type=jnp.float32
    )
    partial_sum = partial_sum + lax.dot_general(
        conv_bf, pieces[1], CONTRACT_LAST, preferred_element_type=jnp.float32
    )
    normed_grad = partial_sum + lax.dot_general(
        dt_bf, pieces[2], CONTRACT_LAST, preferred_element_type=jnp.float32
    )
    unused_input, norm_pull = jax.vjp(input_norm, flat, norm_gain)
    grad_flat, norm_gain_part = norm_pull(normed_grad)
    input_grad = (grad_out.astype(jnp.float32) + grad_flat).reshape(inputs.shape)
    summed = lax.psum(
        (norm_gain_part, grads[3], grads[4], grads[5], grads[6], grads[7], gate_gain_grad),
        ("seq", "span"),
    )
    return (
        output,
        input_grad,
        summed[0],
        z_weight_grad,
        xbc_weight_grad,
        dt_weight_grad,
        summed[1],
        summed[2],
        summed[3],
        summed[4],
        summed[5],
        summed[6],
        out_weight_grad,
    )


def solution(mesh):
    in_specs = (
        P("seq", "span", None),
        P(),
        P(("seq", "span"), None),
        P(("seq", "span"), None),
        P(("seq", "span"), None),
        P(),
        P(),
        P(),
        P(),
        P(),
        P(),
        P(("seq", "span"), None),
        P("seq", "span"),
        P("seq", "span", None),
    )
    out_specs = (
        P("seq", "span", None),
        P("seq", "span", None),
        P(),
        P(("seq", "span"), None),
        P(("seq", "span"), None),
        P(("seq", "span"), None),
        P(),
        P(),
        P(),
        P(),
        P(),
        P(),
        P(("seq", "span"), None),
    )
    return jax.shard_map(body, mesh=mesh, in_specs=in_specs, out_specs=out_specs, check_vma=False)
```

profile of v0, /device:TPU:0, one launch (start us, length us, event | category | flops | bytes accessed | tf_op | source)
XLA Modules:
  0.0 651.5 jit_solution(18130649369982136000)
XLA Ops:
  8.7 2.4 collective-permute-start.1
  12.3 43.7 %all_gather.33 = bf16[768,24]{1,0:T(8,128)(2,1)S(1)} all-gather(bf16[24,24]{1,0:T(8,128)(2,1)} %param.24), channel_id=1, replica_groups=mesh['seq'=8,'span'=4] {'seq','span'}, dimensions={0}, use_global_device_ids=true | all-gather | bytes 38016 | tf_op jit(solution)/shard_map/all_gather | solution.py:152
  63.3 8.4 %all-gather.8.cloned.1.call-done = bf16[768,1792]{1,0:T(8,128)(2,1)} async-done(((bf16[24,1792]{1,0:T(8,128)(2,1)}), bf16[768,1792]{1,0:T(8,128)(2,1)}) %all-gather.8.cloned.1.call-update) | async-done | bytes 2752528 | tf_op jit(solution)/shard_map/all_gather | solution.py:151
  71.7 2.5 convolution_convert_fusion
  74.3 2.1 collective-permute-start
  84.2 6.5 %all_gather.34 = f32[4,1,24]{2,1,0:T(1,128)S(1)} all-gather(f32[1,1,24]{2,1,0:T(1,128)S(1)} %copy.113), channel_id=1, replica_groups=mesh['seq'=8,'span'=4] {'span'}, dimensions={0}, use_global_device_ids=true | all-gather | bytes 480 | tf_op jit(solution)/shard_map/all_gather | solution.py:28
  91.0 19.8 %all-gather.14.cloned.1.call-done = f32[96,64,128]{2,1,0:T(8,128)} async-done(((f32[24,64,128]{2,1,0:T(8,128)}), f32[96,64,128]{2,1,0:T(8,128)}) %all-gather.14.cloned.1.call-update) | async-done | bytes 3145744 | tf_op jit(solution)/shard_map/all_gather | solution.py:28
  111.8 3.3 fusion.19
  115.5 55.3 %all-gather.10.cloned.1.call-done = bf16[768,1536]{1,0:T(8,128)(2,1)} async-done(((bf16[24,1536]{1,0:T(8,128)(2,1)}), bf16[768,1536]{1,0:T(8,128)(2,1)}) %all-gather.10.cloned.1.call-update) | async-done | bytes 2359312 | tf_op jit(solution)/shard_map/all_gather | solution.py:150
  170.8 3.1 multiply_reduce_fusion.11
  174.4 54.9 %all-gather.12.cloned.1.call-done = bf16[1536,768]{1,0:T(8,128)(2,1)} async-done(((bf16[48,768]{1,0:T(8,128)(2,1)}), bf16[1536,768]{1,0:T(8,128)(2,1)}) %all-gather.12.cloned.1.call-update) | async-done | bytes 2359312 | tf_op jit(solution)/shard_map/all_gather | solution.py:191
  229.3 3.4 multiply_reduce_fusion.7
  232.8 2.2 fusion.44
  236.5 2.6 fusion.50
  240.3 2.3 copy.117
  242.6 2.4 mul.724
  245.0 2.4 copy.118
  247.5 4.3 fusion.40
  256.2 10.4 %all-gather.16.cloned.1.call-done = f32[96,64,128]{2,1,0:T(8,128)} async-done(((f32[24,64,128]{2,1,0:T(8,128)}), f32[96,64,128]{2,1,0:T(8,128)}) %all-gather.16.cloned.1.call-update) | async-done | bytes 3145744 | tf_op jit(solution)/shard_map/all_gather | solution.py:28
  266.7 6.2 while.28
  273.7 2.3 multiply_reduce_fusion.6
  277.5 2.8 fusion.13
  280.3 2.4 copy.122
  282.9 2.8 fusion.135
  289.5 2.0 fusion.140
  295.8 2.6 reduce_window_sum.30
  303.1 2.1 fusion.137
  309.4 6.8 %fusion.33 = f32[768,3352]{1,0:T(8,128)} fusion(bf16[128,24]{1,0:T(8,128)(2,1)} %copy.127, bf16[128,1792]{1,0:T(8,128)(2,1)} %scatter-add.4, bf16[128,1536]{1,0:T(8,128)(2,1)} %get-tuple-element.263, bf16[1,128,768]{2,1,0:T(8,128)(2,1)} %param.20, f32[768]{0:T(1024)S(1)} %copy-done.31, f32[128]{0:T(128)S(1)} %copy-done.59), kind=kOutput, calls=%fused_computation.56 | convolution fusion | flops 661997568 | bytes 11355648 | tf_op jit(solution)/shard_map/dot_general | solution.py:244
  317.2 3.1 fusion.80
  328.6 42.0 %all-reduce.15 = (f32[768]{0:T(1024)}, f32[4,1792]{1,0:T(4,128)}, f32[1792]{0:T(1024)}, f32[24]{0:T(128)}, f32[24]{0:T(128)}, /*index=5*/f32[24]{0:T(128)}, f32[1536]{0:T(1024)}) all-reduce(f32[768]{0:T(1024)S(1)} %get-tuple-element.219, f32[4,1792]{1,0:T(4,128)S(1)} %pad_add_fusion.2, ...), channel_id=1, replica_groups=mesh['seq'=8,'span'=4] {'seq','span'}, use_global_device_ids=true, to_apply=%region_18.19 | all-reduce | flops 11336 | bytes 90688 | tf_op jit(solution)/shard_map/psum | solution.py:267
  371.5 160.5 %all-reduce.18.cloned.1.call-done = f32[768,3352]{1,0:T(8,128)} async-done(((f32[768,3352]{1,0:T(8,128)}), f32[768,3352]{1,0:T(8,128)}) %all-reduce.18.cloned.1.call-update) | async-done | bytes 10297360
  536.7 108.0 %reduce-scatter.2.cloned.1.call-done = f32[48,768]{1,0:T(8,128)} async-done(((f32[1536,768]{1,0:T(8,128)}), f32[48,768]{1,0:T(8,128)}) %reduce-scatter.2.cloned.1.call-update) | async-done | bytes 147472 | tf_op jit(solution)/shard_map/reduce_scatter | solution.py:248
  (287 shorter events, 66.3 us)
Async XLA Ops:
  7.2 64.6 %all-gather.8.cloned.1.call-start = ((), (), s32[]{:S(2)}) async-start(), calls=%async_computation.1 | async-start | bytes 2838528 | tf_op jit(solution)/shard_map/all_gather | solution.py:151
  7.9 102.9 %all-gather.14.cloned.1.call-start = ((), (), s32[]{:S(2)}) async-start(), calls=%async_computation.5 | async-start | bytes 3932160 | tf_op jit(solution)/shard_map/all_gather | solution.py:28
  8.7 51.8 %collective-permute-start.1 = (bf16[1,3]{1,0:T(2,128)(2,1)S(1)}, bf16[1,3]{1,0:T(2,128)(2,1)S(1)}, u32[]{:S(2)}, u32[]{:S(2)}) collective-permute-start(bf16[1,3]{1,0:T(2,128)(2,1)S(1)} %add_convert_fusion.1), channel_id=1, source_target_pairs={{0,1},{1,2},{2,3},{4,5},{5,6},{6,7},{8,9},{9,10},{10,11},{12,13},{... | collective-permute-start | bytes 26 | tf_op jit(solution)/shard_map/ppermute | solution.py:21
  57.1 17.1 %copy-start.86 = (f32[128]{0:T(128)}, f32[128]{0:T(128)S(1)}, u32[]{:S(2)}) copy-start(f32[128]{0:T(128)S(1)} %fusion.74) | copy-start | bytes 1540
  57.8 16.4 %copy-start.58 = (f32[128]{0:T(128)}, f32[128]{0:T(128)S(1)}, u32[]{:S(2)}) copy-start(f32[128]{0:T(128)S(1)} %fusion.123) | copy-start | bytes 1540
  60.5 16.8 %copy-start.39 = (f32[1792]{0:T(1024)}, f32[1792]{0:T(1024)S(1)}, u32[]{:S(2)}) copy-start(f32[1792]{0:T(1024)S(1)} %get-tuple-element.221) | copy-start | bytes 21508
  60.5 16.8 %copy-start.41 = (f32[1792]{0:T(1024)}, f32[1792]{0:T(1024)S(1)}, u32[]{:S(2)}) copy-start(f32[1792]{0:T(1024)S(1)} %get-tuple-element.222) | copy-start | bytes 21508
  60.5 16.8 %copy-start.43 = (f32[1792]{0:T(1024)}, f32[1792]{0:T(1024)S(1)}, u32[]{:S(2)}) copy-start(f32[1792]{0:T(1024)S(1)} %get-tuple-element.223) | copy-start | bytes 21508
  60.5 16.8 %copy-start.45 = (f32[1792]{0:T(1024)}, f32[1792]{0:T(1024)S(1)}, u32[]{:S(2)}) copy-start(f32[1792]{0:T(1024)S(1)} %get-tuple-element.224) | copy-start | bytes 21508
  61.2 16.1 %copy-start.72 = (f32[128]{0:T(128)}, f32[128]{0:T(128)S(1)}, u32[]{:S(2)}) copy-start(f32[128]{0:T(128)S(1)} %get-tuple-element.273) | copy-start | bytes 1540
  63.2 19.6 %copy-start.81 = (f32[128]{0:T(128)}, f32[128]{0:T(128)S(1)}, u32[]{:S(2)}) copy-start(f32[128]{0:T(128)S(1)} %get-tuple-element.278) | copy-start | bytes 1540
  63.3 16.3 %copy-start.34 = (f32[128,24]{0,1:T(8,128)}, f32[128,24]{0,1:T(8,128)S(1)}, u32[]{:S(2)}) copy-start(f32[128,24]{0,1:T(8,128)S(1)} %get-tuple-element.269) | copy-start | bytes 36868
  63.3 48.5 %copy-start.36 = (f32[128,24]{0,1:T(8,128)}, f32[128,24]{0,1:T(8,128)S(1)}, u32[]{:S(2)}) copy-start(f32[128,24]{0,1:T(8,128)S(1)} %get-tuple-element.268) | copy-start | bytes 36868
  63.3 48.5 %copy-start.62 = (f32[24,128]{1,0:T(8,128)}, f32[24,128]{1,0:T(8,128)S(1)}, u32[]{:S(2)}) copy-start(f32[24,128]{1,0:T(8,128)S(1)} %get-tuple-element.270) | copy-start | bytes 36868
  74.3 3.0 collective-permute-start
  79.2 31.8 %copy-start.2 = (f32[1,128,1792]{2,1,0:T(8,128)}, f32[1,128,1792]{2,1,0:T(8,128)S(1)}, u32[]{:S(2)}) copy-start(f32[1,128,1792]{2,1,0:T(8,128)S(1)} %get-tuple-element.261) | copy-start | bytes 2752516
  81.2 89.5 %all-gather.10.cloned.1.call-start = ((), (), s32[]{:S(2)}) async-start(), calls=%async_computation.2 | async-start | bytes 2433024 | tf_op jit(solution)/shard_map/all_gather | solution.py:150
  82.0 147.3 %all-gather.12.cloned.1.call-start = ((), (), s32[]{:S(2)}) async-start(), calls=%async_computation.3 | async-start | bytes 2433024 | tf_op jit(solution)/shard_map/all_gather | solution.py:191
  82.6 184.0 %all-gather.16.cloned.1.call-start = ((), (), s32[]{:S(2)}) async-start(), calls=%async_computation.6 | async-start | bytes 3932160 | tf_op jit(solution)/shard_map/all_gather | solution.py:28
  82.7 29.1 %copy-start.60 = (f32[24,128]{1,0:T(8,128)}, f32[24,128]{1,0:T(8,128)S(1)}, u32[]{:S(2)}) copy-start(f32[24,128]{1,0:T(8,128)S(1)} %copy.108) | copy-start | bytes 36868
  82.8 29.0 %copy-start.56 = (pred[128,128]{1,0:T(8,128)(4,1)}, pred[128,128]{1,0:T(8,128)(4,1)S(1)}, u32[]{:S(2)}) copy-start(pred[128,128]{1,0:T(8,128)(4,1)S(1)} %fusion.94) | copy-start | bytes 49156
  91.0 20.8 %copy-start.47 = (f32[128,128]{1,0:T(8,128)}, f32[128,128]{1,0:T(8,128)S(1)}, u32[]{:S(2)}) copy-start(f32[128,128]{1,0:T(8,128)S(1)} %fusion.90) | copy-start | bytes 196612
  115.1 55.6 %copy-start.11 = (bf16[1,128,768]{2,1,0:T(8,128)(2,1)S(1)}, bf16[1,128,768]{2,1,0:T(8,128)(2,1)}, u32[]{:S(2)}) copy-start(bf16[1,128,768]{2,1,0:T(8,128)(2,1)} %param.20) | copy-start | bytes 589828
  115.2 55.6 %copy-start.31 = (f32[768]{0:T(1024)S(1)}, f32[768]{0:T(1024)}, u32[]{:S(2)}) copy-start(f32[768]{0:T(1024)} %param.21) | copy-start | bytes 9220
  115.4 58.4 %copy-start.19 = (f32[128,1536]{1,0:T(8,128)}, f32[128,1536]{1,0:T(8,128)S(1)}, u32[]{:S(2)}) copy-start(f32[128,1536]{1,0:T(8,128)S(1)} %copy.115) | copy-start | bytes 2359300
  115.5 113.8 %copy-start.22 = (bf16[1,128,768]{2,1,0:T(8,128)(2,1)S(1)}, bf16[1,128,768]{2,1,0:T(8,128)(2,1)}, u32[]{:S(2)}) copy-start(bf16[1,128,768]{2,1,0:T(8,128)(2,1)} %param.33) | copy-start | bytes 589828
  174.4 58.4 %copy-start.78 = (f32[128]{0:T(128)}, f32[128]{0:T(128)S(1)}, u32[]{:S(2)}) copy-start(f32[128]{0:T(128)S(1)} %fusion.124) | copy-start | bytes 1540
  236.4 17.6 %copy-start.9 = (f32[128,1536]{0,1:T(8,128)}, f32[128,1536]{0,1:T(8,128)S(1)}, u32[]{:S(2)}) copy-start(f32[128,1536]{0,1:T(8,128)S(1)} %copy.119) | copy-start | bytes 2359300
  239.1 292.9 %all-reduce.18.cloned.1.call-start = ((), (), s32[]{:S(2)}) async-start(), calls=%async_computation.7 | async-start | bytes 21233664
  299.9 6.7 %collective-permute-start.2 = (f32[1,3,1792]{2,1,0:T(4,128)}, f32[1,3,1792]{2,1,0:T(4,128)}, u32[]{:S(2)}, u32[]{:S(2)}) collective-permute-start(f32[1,3,1792]{2,1,0:T(4,128)} %pad_add_fusion.1), channel_id=1, source_target_pairs={{1,0},{2,1},{3,2},{5,4},{6,5},{7,6},{9,8},{10,9},{11,10},{13,12},{... | collective-permute-start | bytes 64520 | tf_op jit(solution)/shard_map/ppermute | solution.py:21
  316.3 328.4 %reduce-scatter.2.cloned.1.call-start = ((), (), s32[]{:S(2)}) async-start(), calls=%async_computation.4 | async-start | bytes 4866048 | tf_op jit(solution)/shard_map/reduce_scatter | solution.py:248
  327.1 43.5 %copy-start.87 = (f32[128]{0:T(128)S(1)}, f32[128]{0:T(128)}, u32[]{:S(2)}) copy-start(f32[128]{0:T(128)} %copy-done.86) | copy-start | bytes 1540
  (71 other events, 269.0 us)
Sparse Core Ops, SparseCore 0:
  10.9 60.8 all-gather.7
  81.4 29.4 all-gather.13
  113.7 56.9 all-gather.9
  173.5 55.7 all-gather.11
  239.2 27.2 all-gather.15
  316.4 215.5 all-reduce.17
  538.1 106.5 reduce-scatter.1
where the time goes:
time: 653 us; the launch traced here: 652 us
  waiting for transfers between devices  420 us (64%)
  blocking collectives  92.2 us (14%)
  matrix products  47.6 us (7%)
  other arithmetic  35.4 us (5%)
  local copies, waits for them, and re-layouts  34.1 us (5%)
  between operations  15.4 us (2%)
  starting transfers between devices  6.53 us (1%)
    unnamed x8, waiting for transfers between devices  162 us
    reduce_scatter x1, waiting for transfers between devices, body(): lax.psum_scatter(out_full, ('seq', 'span'), scatter_dimension=0, tiled=True)  108 us
    all_gather x1, waiting for transfers between devices, body(): lax.all_gather(z_weight, ('seq', 'span'), axis=0, tiled=True)  55.3 us
    all_gather x1, waiting for transfers between devices, body(): lax.all_gather(out_weight, ('seq', 'span'), axis=0, tiled=True)  54.9 us
    all_gather x1, blocking collectives, body(): lax.all_gather(dt_weight, ('seq', 'span'), axis=0, tiled=True)  43.7 us
    psum x1, blocking collectives, body(): lax.psum((norm_gain_part, grads[3], grads[4], grads[5], grads[6], grads[7...  42 us
    all_gather x2, waiting for transfers between devices, carried_in(): gathered = jax.tree.map(lambda a: lax.all_gather(a, axis), part)  30.2 us
  transfers between devices with their start and end apart: 10, of which 8 were waited for; matrix products, arithmetic and copies ran while one was open for 9% of the time, Pallas kernels for 0%

commit v1 on v0

--- a/solution.py
+++ b/solution.py
@@ -13,6 +13,28 @@
 HIGHEST = lax.Precision.HIGHEST
 CONTRACT_LAST = (((1,), (1,)), ((), ()))
 CONTRACT_FIRST = (((0,), (0,)), ((), ()))
+
+
+def laid_out(blocks, dim):
+    blocks = jnp.moveaxis(blocks, 0, dim)
+    lengths = blocks.shape
+    return blocks.reshape(*lengths[:dim], lengths[dim] * lengths[dim + 1], *lengths[dim + 2 :])
+
+
+def collected_by_bits(x, axis):
+    peers = lax.axis_size(axis)
+    blocks = x[None]
+    for level in range(peers.bit_length() - 1):
+        bit = 1 << level
+        theirs = lax.ppermute(blocks, axis, [(i, i ^ bit) for i in range(peers)])
+        both = jnp.stack([blocks, theirs])
+        upper = lax.axis_index(axis) >> level & 1
+        blocks = jnp.where(upper == 0, both, both[::-1]).reshape(-1, *x.shape)
+    return blocks
+
+
+def collect(x, axis, dim):
+    return laid_out(collected_by_bits(x, axis), dim)
 
 
 def shifted(x, axis, by):
@@ -187,9 +209,7 @@
     mix_bf = gated_norm(mixed, gate, gate_gain).astype(jnp.bfloat16)
     columns = mix_bf
     projected = jnp.dot(
-        columns,
-        lax.all_gather(out_weight, ("seq", "span"), axis=0, tiled=True),
-        preferred_element_type=jnp.float32,
+        columns, collect(out_weight, ("seq", "span"), 0), preferred_element_type=jnp.float32
     )
     output = (flat + projected).astype(jnp.bfloat16).reshape(inputs.shape)
     grad_out = cotangent.reshape(rows, width)

time: 653 us -> 707 us (1.083)
  waiting for transfers between devices: 420 us -> 465 us
  starting transfers between devices: 6.53 us -> 14.2 us
    ppermute x0 -> x5, waiting for transfers between devices: none -> 111 us  [collected_by_bits(): theirs = lax.ppermute(blocks, axis, [(i, i ^ bit) for i in range(peers)])]
    unnamed x8, waiting for transfers between devices: 162 us -> 97.5 us
    ppermute x0 -> x5, starting transfers between devices: none -> 7.62 us  [collected_by_bits(): theirs = lax.ppermute(blocks, axis, [(i, i ^ bit) for i in range(peers)])]
  transfers between devices with their start and end apart: 10 -> 15, of which waited for: 8 -> 13; matrix products, arithmetic and copies ran while one was open for 9% -> 8% of each run, Pallas kernels for 0% -> 0%
where the time goes in v1:
time: 707 us; the launch traced here: 705 us
  waiting for transfers between devices  465 us (66%)
  blocking collectives  90.1 us (13%)
  matrix products  46.7 us (7%)
  other arithmetic  36.7 us (5%)
  local copies, waits for them, and re-layouts  36.3 us (5%)
  between operations  15.4 us (2%)
  starting transfers between devices  14.2 us (2%)
    ppermute x5, waiting for transfers between devices, collected_by_bits(): theirs = lax.ppermute(blocks, axis, [(i, i ^ bit) for i in range(peers)])  111 us
    reduce_scatter x1, waiting for transfers between devices, body(): lax.psum_scatter(out_full, ('seq', 'span'), scatter_dimension=0, tiled=True)  108 us
    unnamed x8, waiting for transfers between devices  97.5 us
    all_gather x1, waiting for transfers between devices, body(): lax.all_gather(out_weight, ('seq', 'span'), axis=0, tiled=True)  55.2 us
    all_gather x1, waiting for transfers between devices, body(): lax.all_gather(z_weight, ('seq', 'span'), axis=0, tiled=True)  54.4 us
    all_gather x1, blocking collectives, body(): lax.all_gather(dt_weight, ('seq', 'span'), axis=0, tiled=True)  43.7 us
    psum x1, blocking collectives, body(): lax.psum((norm_gain_part, grads[3], grads[4], grads[5], grads[6], grads[7...  39.9 us
    all_gather x2, waiting for transfers between devices, carried_in(): gathered = jax.tree.map(lambda a: lax.all_gather(a, axis), part)  30.8 us
  transfers between devices with their start and end apart: 15, of which 13 were waited for; matrix products, arithmetic and copies ran while one was open for 8% of the time, Pallas kernels for 0%

profile of v1, /device:TPU:0, one launch (start us, length us, event | category | flops | bytes accessed | tf_op | source)
XLA Modules:
  0.0 705.1 jit_solution(8547581576306912661)
XLA Ops:
  8.7 2.4 collective-permute-start.1
  12.3 43.7 %all_gather.32 = bf16[768,24]{1,0:T(8,128)(2,1)S(1)} all-gather(bf16[24,24]{1,0:T(8,128)(2,1)} %param.24), channel_id=1, replica_groups=mesh['seq'=8,'span'=4] {'seq','span'}, dimensions={0}, use_global_device_ids=true | all-gather | bytes 38016 | tf_op jit(solution)/shard_map/all_gather | solution.py:174
  63.8 7.9 %all-gather.8.cloned.1.call-done = bf16[768,1792]{1,0:T(8,128)(2,1)} async-done(((bf16[24,1792]{1,0:T(8,128)(2,1)}), bf16[768,1792]{1,0:T(8,128)(2,1)}) %all-gather.8.cloned.1.call-update) | async-done | bytes 2752528 | tf_op jit(solution)/shard_map/all_gather | solution.py:173
  71.7 2.5 convolution_convert_fusion
  84.2 6.5 all_gather.33
  91.0 19.8 %all-gather.14.cloned.1.call-done = f32[96,64,128]{2,1,0:T(8,128)} async-done(((f32[24,64,128]{2,1,0:T(8,128)}), f32[96,64,128]{2,1,0:T(8,128)}) %all-gather.14.cloned.1.call-update) | async-done | bytes 3145744 | tf_op jit(solution)/shard_map/all_gather | solution.py:50
  111.8 3.3 fusion.19
  116.3 54.4 %all-gather.10.cloned.1.call-done = bf16[768,1536]{1,0:T(8,128)(2,1)} async-done(((bf16[24,1536]{1,0:T(8,128)(2,1)}), bf16[768,1536]{1,0:T(8,128)(2,1)}) %all-gather.10.cloned.1.call-update) | async-done | bytes 2359312 | tf_op jit(solution)/shard_map/all_gather | solution.py:172
  170.8 3.3 multiply_reduce_fusion.11
  174.1 55.2 %all-gather.12.cloned.1.call-done = bf16[1536,768]{1,0:T(8,128)(2,1)} async-done(((bf16[48,768]{1,0:T(8,128)(2,1)}), bf16[1536,768]{1,0:T(8,128)(2,1)}) %all-gather.12.cloned.1.call-update) | async-done | bytes 2359312 | tf_op jit(solution)/shard_map/all_gather | solution.py:218
  229.3 3.5 multiply_reduce_fusion.7
  237.3 2.8 fusion.50
  243.5 2.4 mul.732
  246.0 2.4 copy.118
  248.4 5.6 fusion.40
  256.6 11.0 %all-gather.16.cloned.1.call-done = f32[96,64,128]{2,1,0:T(8,128)} async-done(((f32[24,64,128]{2,1,0:T(8,128)}), f32[96,64,128]{2,1,0:T(8,128)}) %all-gather.16.cloned.1.call-update) | async-done | bytes 3145744 | tf_op jit(solution)/shard_map/all_gather | solution.py:50
  267.6 6.2 while.28
  274.7 2.3 multiply_reduce_fusion.6
  278.5 2.8 fusion.13
  281.4 2.4 copy.122
  283.9 2.8 fusion.137
  296.9 2.6 reduce_window_sum.30
  310.5 6.8 fusion.33
  320.4 3.1 fusion.80
  323.5 4.2 collective-permute-done.3
  329.4 11.8 %collective-permute-done.4 = bf16[4,48,768]{2,1,0:T(8,128)(2,1)S(1)} collective-permute-done((bf16[4,48,768]{2,1,0:T(8,128)(2,1)S(1)}, bf16[4,48,768]{2,1,0:T(8,128)(2,1)S(1)}, u32[]{:S(2)}, u32[]{:S(2)}) %collective-permute-start.4) | collective-permute-done | bytes 294944 | tf_op jit(solution)/shard_map/ppermute | solution.py:29
  342.9 25.9 %collective-permute-done.5 = bf16[8,48,768]{2,1,0:T(8,128)(2,1)S(1)} collective-permute-done((bf16[8,48,768]{2,1,0:T(8,128)(2,1)S(1)}, bf16[8,48,768]{2,1,0:T(8,128)(2,1)S(1)}, u32[]{:S(2)}, u32[]{:S(2)}) %collective-permute-start.5) | collective-permute-done | bytes 589856 | tf_op jit(solution)/shard_map/ppermute | solution.py:29
  369.2 3.3 collective-permute-start.6
  372.5 67.9 %collective-permute-done.6 = bf16[16,48,768]{2,1,0:T(8,128)(2,1)S(1)} collective-permute-done((bf16[16,48,768]{2,1,0:T(8,128)(2,1)S(1)}, bf16[16,48,768]{2,1,0:T(8,128)(2,1)S(1)}, u32[]{:S(2)}, u32[]{:S(2)}) %collective-permute-start.6) | collective-permute-done | bytes 1179680 | tf_op jit(solution)/shard_map/ppermute | solution.py:29
  449.1 39.9 %all-reduce.15 = (f32[768]{0:T(1024)}, f32[4,1792]{1,0:T(4,128)}, f32[1792]{0:T(1024)}, f32[24]{0:T(128)}, f32[24]{0:T(128)}, /*index=5*/f32[24]{0:T(128)}, f32[1536]{0:T(1024)}) all-reduce(f32[768]{0:T(1024)S(1)} %get-tuple-element.219, f32[4,1792]{1,0:T(4,128)S(1)} %pad_add_fusion.2, ...), channel_id=1, replica_groups=mesh['seq'=8,'span'=4] {'seq','span'}, use_global_device_ids=true, to_apply=%region_18.19 | all-reduce | flops 11336 | bytes 90688 | tf_op jit(solution)/shard_map/psum | solution.py:287
  490.0 95.6 %all-reduce.18.cloned.1.call-done = f32[768,3352]{1,0:T(8,128)} async-done(((f32[768,3352]{1,0:T(8,128)}), f32[768,3352]{1,0:T(8,128)}) %all-reduce.18.cloned.1.call-update) | async-done | bytes 10297360
  590.2 108.0 %reduce-scatter.2.cloned.1.call-done = f32[48,768]{1,0:T(8,128)} async-done(((f32[1536,768]{1,0:T(8,128)}), f32[48,768]{1,0:T(8,128)}) %reduce-scatter.2.cloned.1.call-update) | async-done | bytes 147472 | tf_op jit(solution)/shard_map/reduce_scatter | solution.py:268
  (301 shorter events, 83.2 us)
Async XLA Ops:
  7.2 64.6 %all-gather.8.cloned.1.call-start = ((), (), s32[]{:S(2)}) async-start(), calls=%async_computation.1 | async-start | bytes 2838528 | tf_op jit(solution)/shard_map/all_gather | solution.py:173
  7.9 102.9 %all-gather.14.cloned.1.call-start = ((), (), s32[]{:S(2)}) async-start(), calls=%async_computation.5 | async-start | bytes 3932160 | tf_op jit(solution)/shard_map/all_gather | solution.py:50
  8.7 51.8 %collective-permute-start.1 = (bf16[1,3]{1,0:T(2,128)(2,1)S(1)}, bf16[1,3]{1,0:T(2,128)(2,1)S(1)}, u32[]{:S(2)}, u32[]{:S(2)}) collective-permute-start(bf16[1,3]{1,0:T(2,128)(2,1)S(1)} %add_convert_fusion.1), channel_id=1, source_target_pairs={{0,1},{1,2},{2,3},{4,5},{5,6},{6,7},{8,9},{9,10},{10,11},{12,13},{... | collective-permute-start | bytes 26 | tf_op jit(solution)/shard_map/ppermute | solution.py:43
  57.1 17.1 %copy-start.85 = (f32[128]{0:T(128)}, f32[128]{0:T(128)S(1)}, u32[]{:S(2)}) copy-start(f32[128]{0:T(128)S(1)} %fusion.74) | copy-start | bytes 1540
  57.8 112.9 %copy-start.54 = (f32[128]{0:T(128)}, f32[128]{0:T(128)S(1)}, u32[]{:S(2)}) copy-start(f32[128]{0:T(128)S(1)} %fusion.125) | copy-start | bytes 1540
  60.5 16.8 %copy-start.34 = (f32[1792]{0:T(1024)}, f32[1792]{0:T(1024)S(1)}, u32[]{:S(2)}) copy-start(f32[1792]{0:T(1024)S(1)} %get-tuple-element.221) | copy-start | bytes 21508
  61.2 18.0 %copy-start.65 = (f32[128]{0:T(128)}, f32[128]{0:T(128)S(1)}, u32[]{:S(2)}) copy-start(f32[128]{0:T(128)S(1)} %get-tuple-element.273) | copy-start | bytes 1540
  61.2 18.0 %copy-start.68 = (f32[128]{0:T(128)}, f32[128]{0:T(128)S(1)}, u32[]{:S(2)}) copy-start(f32[128]{0:T(128)S(1)} %get-tuple-element.274) | copy-start | bytes 1540
  61.2 18.0 %copy-start.71 = (f32[128]{0:T(128)}, f32[128]{0:T(128)S(1)}, u32[]{:S(2)}) copy-start(f32[128]{0:T(128)S(1)} %get-tuple-element.275) | copy-start | bytes 1540
  63.2 19.6 %copy-start.80 = (f32[128]{0:T(128)}, f32[128]{0:T(128)S(1)}, u32[]{:S(2)}) copy-start(f32[128]{0:T(128)S(1)} %get-tuple-element.280) | copy-start | bytes 1540
  63.8 48.0 %copy-start.60 = (f32[24,128]{1,0:T(8,128)}, f32[24,128]{1,0:T(8,128)S(1)}, u32[]{:S(2)}) copy-start(f32[24,128]{1,0:T(8,128)S(1)} %get-tuple-element.272) | copy-start | bytes 36868
  74.3 3.0 collective-permute-start
  79.1 175.1 %copy-start.2 = (f32[1,128,1792]{2,1,0:T(8,128)}, f32[1,128,1792]{2,1,0:T(8,128)S(1)}, u32[]{:S(2)}) copy-start(f32[1,128,1792]{2,1,0:T(8,128)S(1)} %get-tuple-element.261) | copy-start | bytes 2752516
  81.2 89.5 %all-gather.10.cloned.1.call-start = ((), (), s32[]{:S(2)}) async-start(), calls=%async_computation.2 | async-start | bytes 2433024 | tf_op jit(solution)/shard_map/all_gather | solution.py:172
  82.0 147.3 %all-gather.12.cloned.1.call-start = ((), (), s32[]{:S(2)}) async-start(), calls=%async_computation.3 | async-start | bytes 2433024 | tf_op jit(solution)/shard_map/all_gather | solution.py:218
  82.5 185.0 %all-gather.16.cloned.1.call-start = ((), (), s32[]{:S(2)}) async-start(), calls=%async_computation.6 | async-start | bytes 3932160 | tf_op jit(solution)/shard_map/all_gather | solution.py:50
  82.7 29.1 %copy-start.57 = (f32[24,128]{1,0:T(8,128)}, f32[24,128]{1,0:T(8,128)S(1)}, u32[]{:S(2)}) copy-start(f32[24,128]{1,0:T(8,128)S(1)} %copy.108) | copy-start | bytes 36868
  82.8 165.5 %copy-start.52 = (pred[128,128]{1,0:T(8,128)(4,1)}, pred[128,128]{1,0:T(8,128)(4,1)S(1)}, u32[]{:S(2)}) copy-start(pred[128,128]{1,0:T(8,128)(4,1)S(1)} %fusion.96) | copy-start | bytes 49156
  91.0 20.8 %copy-start.42 = (f32[128,128]{1,0:T(8,128)}, f32[128,128]{1,0:T(8,128)S(1)}, u32[]{:S(2)}) copy-start(f32[128,128]{1,0:T(8,128)S(1)} %fusion.92) | copy-start | bytes 196612
  115.1 55.6 %copy-start.9 = (bf16[1,128,768]{2,1,0:T(8,128)(2,1)S(1)}, bf16[1,128,768]{2,1,0:T(8,128)(2,1)}, u32[]{:S(2)}) copy-start(bf16[1,128,768]{2,1,0:T(8,128)(2,1)} %param.20) | copy-start | bytes 589828
  115.1 55.6 %copy-start.28 = (f32[768]{0:T(1024)S(1)}, f32[768]{0:T(1024)}, u32[]{:S(2)}) copy-start(f32[768]{0:T(1024)} %param.21) | copy-start | bytes 9220
  116.3 113.0 %copy-start.29 = (f32[1536]{0:T(1024)S(1)}, f32[1536]{0:T(1024)}, u32[]{:S(2)}) copy-start(f32[1536]{0:T(1024)} %param.30) | copy-start | bytes 18436
  174.1 58.7 %copy-start.77 = (f32[128]{0:T(128)}, f32[128]{0:T(128)S(1)}, u32[]{:S(2)}) copy-start(f32[128]{0:T(128)S(1)} %fusion.126) | copy-start | bytes 1540
  240.1 345.5 %all-reduce.18.cloned.1.call-start = ((), (), s32[]{:S(2)}) async-start(), calls=%async_computation.7 | async-start | bytes 21233664
  300.9 6.7 collective-permute-start.7
  317.3 380.9 %reduce-scatter.2.cloned.1.call-start = ((), (), s32[]{:S(2)}) async-start(), calls=%async_computation.4 | async-start | bytes 4866048 | tf_op jit(solution)/shard_map/reduce_scatter | solution.py:268
  318.2 2.0 collective-permute-start.2
  320.3 7.5 %collective-permute-start.3 = (bf16[2,48,768]{2,1,0:T(8,128)(2,1)S(1)}, bf16[2,48,768]{2,1,0:T(8,128)(2,1)S(1)}, u32[]{:S(2)}, u32[]{:S(2)}) collective-permute-start(bf16[2,48,768]{2,1,0:T(8,128)(2,1)S(1)} %get-tuple-element.269), channel_id=1, source_target_pairs={{0,2},{1,3},{2,0},{3,1},{4,6},{5,7},{6,4},{7,5},{8,10},{9,11},{10,... | collective-permute-start | bytes 442376 | tf_op jit(solution)/shard_map/ppermute | solution.py:29
  327.8 13.4 %collective-permute-start.4 = (bf16[4,48,768]{2,1,0:T(8,128)(2,1)S(1)}, bf16[4,48,768]{2,1,0:T(8,128)(2,1)S(1)}, u32[]{:S(2)}, u32[]{:S(2)}) collective-permute-start(bf16[4,48,768]{2,1,0:T(8,128)(2,1)S(1)} %bitcast.299), channel_id=1, source_target_pairs={{0,4},{1,5},{2,6},{3,7},{4,0},{5,1},{6,2},{7,3},{8,12},{9,13},{10,... | collective-permute-start | bytes 884744 | tf_op jit(solution)/shard_map/ppermute | solution.py:29
  341.4 27.5 %collective-permute-start.5 = (bf16[8,48,768]{2,1,0:T(8,128)(2,1)S(1)}, bf16[8,48,768]{2,1,0:T(8,128)(2,1)S(1)}, u32[]{:S(2)}, u32[]{:S(2)}) collective-permute-start(bf16[8,48,768]{2,1,0:T(8,128)(2,1)S(1)} %bitcast.297), channel_id=1, source_target_pairs={{0,8},{1,9},{2,10},{3,11},{4,12},{5,13},{6,14},{7,15},{8,0},{9,1},... | collective-permute-start | bytes 1769480 | tf_op jit(solution)/shard_map/ppermute | solution.py:29
  369.2 71.2 %collective-permute-start.6 = (bf16[16,48,768]{2,1,0:T(8,128)(2,1)S(1)}, bf16[16,48,768]{2,1,0:T(8,128)(2,1)S(1)}, u32[]{:S(2)}, u32[]{:S(2)}) collective-permute-start(bf16[16,48,768]{2,1,0:T(8,128)(2,1)S(1)} %bitcast.293), channel_id=1, source_target_pairs={{0,16},{1,17},{2,18},{3,19},{4,20},{5,21},{6,22},{7,23},{8,24},{9,... | collective-permute-start | bytes 3538952 | tf_op jit(solution)/shard_map/ppermute | solution.py:29
  447.7 41.4 %copy-start.86 = (f32[128]{0:T(128)S(1)}, f32[128]{0:T(128)}, u32[]{:S(2)}) copy-start(f32[128]{0:T(128)} %copy-done.85) | copy-start | bytes 1540
  (73 other events, 304.5 us)
Sparse Core Ops, SparseCore 0:
  10.9 60.8 all-gather.7
  81.3 29.4 all-gather.13
  113.7 56.9 all-gather.9
  173.5 55.7 all-gather.11
  240.2 27.2 all-gather.15
  317.4 268.0 all-reduce.17
  591.6 106.5 reduce-scatter.1
